TPU v7x, 256 devices: a whole 4x4x8 slice. The times are simulated.
256 devices in a mesh: segment: 2 (over core), angle: 16 (over x_lo, z), tile: 8 (over y, x_hi).
Axes of the slice: x: 4 (x_hi: 2, x_lo: 2; x = x_hi * 2 + x_lo), y: 4, z: 8, core: 2. Of those that a mesh axis runs over, the one named last changes fastest.
Arguments:
- sinogram: float32 [64, 32, 4096], P(('segment', 'angle'), 'tile'), may hold values from -6 to 6
- paganin_width: float32 [1], replicated, may hold values from 2 to 8
- window_block: int32 [64, 8], replicated, may hold values from 0 to 28
Outputs:
- volume: float32 [8, 32, 65536], P('tile', None, ('segment', 'angle'))
All inputs are finite; a program needn't handle non-finite values.
Results may differ from a plain program's by a relative error of at most 0.0035.
Values may be sent and summed in bfloat16 or wider, within the bound.
A program may use at most 64 MiB of HBM per device.

v0:
```python
import math
import jax
import jax.numpy as jnp
from jax import lax
from jax.sharding import PartitionSpec as P

WIN = 512
BAND = 128
ROWS_DEV = 8
TCOLS = 256


def band_kernels(width):
    inner = jnp.arange(128, dtype=jnp.int32)
    offsets = (
        (jnp.arange(3, dtype=jnp.int32) - 1)[:, None, None] * 128
        + inner[None, :, None]
        - inner[None, None, :]
    )
    spread = offsets.astype(jnp.float32)
    inside = jnp.abs(offsets) <= BAND
    taps = jnp.arange(-BAND, BAND + 1).astype(jnp.float32)
    normal_total = jnp.sum(jnp.exp(-jnp.abs(taps) / width))
    paganin = jnp.where(inside, jnp.exp(-jnp.abs(spread) / width) / normal_total, 0.0)
    squared = jnp.maximum(spread * spread, 1.0)
    odd_taps = jnp.where(inside & (offsets % 2 == 1), -1.0 / (math.pi * math.pi * squared), 0.0)
    ramp = jnp.where(offsets == 0, 0.25, odd_taps)
    return (paganin, ramp)


def apply_band(rows, kernels):
    row_count, bins = rows.shape
    blocks = bins // 128
    shaped = rows.reshape(row_count, blocks, 128)
    padded = jnp.pad(shaped, ((0, 0), (1, 1), (0, 0)))
    result = jnp.zeros_like(shaped)
    for offset in range(3):
        result = result + jnp.einsum(
            "rbi,io->rbo",
            padded[:, offset : offset + blocks],
            kernels[offset],
            precision=lax.Precision.HIGHEST,
        )
    return result.reshape(row_count, bins)


def hat_block(angles, angle_total, row_first, row_count, tile_rows):
    theta = math.pi * angles.astype(jnp.float32) / angle_total
    rows_here = (row_first + jnp.arange(row_count, dtype=jnp.int32)).astype(jnp.float32) - (
        tile_rows - 1
    ) / 2.0
    columns = jnp.arange(TCOLS).astype(jnp.float32) - (TCOLS - 1) / 2.0
    across = (
        columns[None, None, :] * jnp.cos(theta)[:, None, None]
        + rows_here[None, :, None] * jnp.sin(theta)[:, None, None]
    )
    across = across.reshape(angles.shape[0], row_count * TCOLS) + WIN / 2.0
    detector = jnp.arange(WIN).astype(jnp.float32)
    weight = jnp.maximum(0.0, 1.0 - jnp.abs(across[:, None, :] - detector[None, :, None]))
    return weight.astype(jnp.bfloat16)


def accumulate_rows(total, piece, starts, row_first, angle_total, tile_rows):
    count = piece.shape[0]
    group = math.gcd(count, 4)
    turns = count // group
    blocks = piece.reshape(turns, group, piece.shape[1], piece.shape[2])
    start_groups = starts.reshape(turns, group)

    def advance(carry, item):
        block, window_starts, index = item
        angles = index * group + jnp.arange(group, dtype=jnp.int32)
        weights = hat_block(angles, angle_total, row_first, ROWS_DEV, tile_rows)
        for member in range(group):
            window = lax.dynamic_slice_in_dim(block[member], window_starts[member], WIN, 1)
            carry = carry + jnp.dot(window, weights[member], preferred_element_type=jnp.float32)
        return (carry, None)

    result, ignored = lax.scan(
        advance, total, (blocks, start_groups, jnp.arange(turns, dtype=jnp.int32))
    )
    return result


def body(sinogram, paganin_width, window_block):
    angle_local, slice_local, bins = sinogram.shape
    group_size = lax.axis_size(("segment", "angle"))
    tile_count = lax.axis_size("tile")
    angle_total = angle_local * group_size
    tile_rows = ROWS_DEV * group_size
    position = lax.axis_index(("segment", "angle"))
    tile_index = lax.axis_index("tile")
    row_first = position * ROWS_DEV
    smoothing, ramping = band_kernels(paganin_width[0])
    rows = sinogram.reshape(angle_local * slice_local, bins)
    filtered = (
        apply_band(apply_band(rows, smoothing), ramping)
        .astype(jnp.bfloat16)
        .reshape(angle_local, slice_local, bins)
    )
    slice_total = slice_local * tile_count
    empty = jnp.zeros((slice_total, ROWS_DEV * TCOLS), jnp.float32)
    own_starts = lax.dynamic_slice_in_dim(window_block, tile_index, 1, 1)[:, 0] * 128
    slab = lax.all_gather(filtered, "tile", axis=1, tiled=True)
    volume = accumulate_rows(
        empty,
        lax.all_gather(slab, ("segment", "angle"), axis=0, tiled=True),
        own_starts,
        row_first,
        angle_total,
        tile_rows,
    )
    return volume[None]


def solution(mesh):
    in_specs = (P(("segment", "angle"), "tile", None), P(), P())
    out_specs = P("tile", None, ("segment", "angle"))
    return jax.shard_map(body, mesh=mesh, in_specs=in_specs, out_specs=out_specs, check_vma=False)
```

profile of v0, /device:TPU:1, one launch (start us, length us, event | category | flops | bytes accessed | tf_op | source)
XLA Modules:
  0.0 552.1 jit_solution(8481169078443803155)
XLA Ops:
  11.6 31.7 %all_gather.6 = bf16[2,32,4096]{2,0,1:T(2,128)(2,1)S(1)} all-gather(bf16[2,4,4096]{2,0,1:T(2,128)(2,1)S(1)} %copy.6), channel_id=1, replica_groups=mesh['segment'=2,'angle'=16,'tile'=8] {'tile'}, dimensions={1}, use_global_device_ids=true | all-gather | bytes 589824 | tf_op jit(solution)/shard_map/all_gather | solution.py:104
  45.2 107.4 %all-gather.2.cloned.1.call-done = bf16[64,32,4096]{2,1,0:T(8,128)(2,1)} async-done(((bf16[2,32,4096]{2,1,0:T(8,128)(2,1)}), bf16[64,32,4096]{2,1,0:T(8,128)(2,1)}) %all-gather.2.cloned.1.call-update) | async-done | bytes 16777232 | tf_op jit(solution)/shard_map/all_gather | solution.py:107
  152.6 392.0 %while.14 = (s32[]{:T(128)}, f32[32,2048]{1,0:T(8,128)S(1)}, bf16[16,4,32,4096]{3,2,1,0:T(8,128)(2,1)}, s32[16,4]{1,0:T(8,128)S(1)}, s32[16]{0:T(128)S(1)}, /*in...) while((s32[]{:T(128)}, f32[32,2048]{1,0:T(8,128)S(1)}, ...), condition=%wide.region_2.3_spmd.clone, body=%wide.region_1.2_spmd.clone.sunk | while | flops 289753152 | bytes 19153716 | solution.py:79
  156.7 6.2 %maximum_convert_fusion.2 = bf16[4,512,2048]{2,1,0:T(8,128)(2,1)} fusion(f32[512]{0:T(512)S(1)} %iota_convert_fusion.2, f32[4,2048]{1,0:T(4,128)S(1)} %bitcast.105), kind=kLoop, calls=%fused_computation.clone.1 | loop fusion | flops 20971520 | bytes 8423424 | tf_op jit(solution)/shard_map/while/body/eval_jaxpr/convert_element_type | solution.py:60
  170.7 2.1 convolution_add_fusion.13
  181.2 6.2 %maximum_convert_fusion.2 = bf16[4,512,2048]{2,1,0:T(8,128)(2,1)} fusion(f32[512]{0:T(512)S(1)} %iota_convert_fusion.2, f32[4,2048]{1,0:T(4,128)S(1)} %bitcast.105), kind=kLoop, calls=%fused_computation.clone.1 | loop fusion | flops 20971520 | bytes 8423424 | tf_op jit(solution)/shard_map/while/body/eval_jaxpr/convert_element_type | solution.py:60
  191.4 2.1 convolution_add_fusion.12
  195.2 2.1 convolution_add_fusion.13
  199.4 2.1 convolution_add_fusion.14
  205.7 6.2 %maximum_convert_fusion.2 = bf16[4,512,2048]{2,1,0:T(8,128)(2,1)} fusion(f32[512]{0:T(512)S(1)} %iota_convert_fusion.2, f32[4,2048]{1,0:T(4,128)S(1)} %bitcast.105), kind=kLoop, calls=%fused_computation.clone.1 | loop fusion | flops 20971520 | bytes 8423424 | tf_op jit(solution)/shard_map/while/body/eval_jaxpr/convert_element_type | solution.py:60
  219.7 2.1 convolution_add_fusion.13
  230.2 6.2 %maximum_convert_fusion.2 = bf16[4,512,2048]{2,1,0:T(8,128)(2,1)} fusion(f32[512]{0:T(512)S(1)} %iota_convert_fusion.2, f32[4,2048]{1,0:T(4,128)S(1)} %bitcast.105), kind=kLoop, calls=%fused_computation.clone.1 | loop fusion | flops 20971520 | bytes 8423424 | tf_op jit(solution)/shard_map/while/body/eval_jaxpr/convert_element_type | solution.py:60
  240.5 2.1 convolution_add_fusion.12
  244.2 2.1 convolution_add_fusion.13
  254.7 6.2 %maximum_convert_fusion.2 = bf16[4,512,2048]{2,1,0:T(8,128)(2,1)} fusion(f32[512]{0:T(512)S(1)} %iota_convert_fusion.2, f32[4,2048]{1,0:T(4,128)S(1)} %bitcast.105), kind=kLoop, calls=%fused_computation.clone.1 | loop fusion | flops 20971520 | bytes 8423424 | tf_op jit(solution)/shard_map/while/body/eval_jaxpr/convert_element_type | solution.py:60
  265.0 2.1 convolution_add_fusion.12
  272.9 2.1 convolution_add_fusion.14
  279.2 6.2 %maximum_convert_fusion.2 = bf16[4,512,2048]{2,1,0:T(8,128)(2,1)} fusion(f32[512]{0:T(512)S(1)} %iota_convert_fusion.2, f32[4,2048]{1,0:T(4,128)S(1)} %bitcast.105), kind=kLoop, calls=%fused_computation.clone.1 | loop fusion | flops 20971520 | bytes 8423424 | tf_op jit(solution)/shard_map/while/body/eval_jaxpr/convert_element_type | solution.py:60
  289.5 2.1 convolution_add_fusion.12
  293.3 2.1 convolution_add_fusion.13
  297.4 2.1 convolution_add_fusion.14
  303.7 6.2 %maximum_convert_fusion.2 = bf16[4,512,2048]{2,1,0:T(8,128)(2,1)} fusion(f32[512]{0:T(512)S(1)} %iota_convert_fusion.2, f32[4,2048]{1,0:T(4,128)S(1)} %bitcast.105), kind=kLoop, calls=%fused_computation.clone.1 | loop fusion | flops 20971520 | bytes 8423424 | tf_op jit(solution)/shard_map/while/body/eval_jaxpr/convert_element_type | solution.py:60
  317.8 2.1 convolution_add_fusion.13
  328.2 6.2 %maximum_convert_fusion.2 = bf16[4,512,2048]{2,1,0:T(8,128)(2,1)} fusion(f32[512]{0:T(512)S(1)} %iota_convert_fusion.2, f32[4,2048]{1,0:T(4,128)S(1)} %bitcast.105), kind=kLoop, calls=%fused_computation.clone.1 | loop fusion | flops 20971520 | bytes 8423424 | tf_op jit(solution)/shard_map/while/body/eval_jaxpr/convert_element_type | solution.py:60
  338.5 2.1 convolution_add_fusion.12
  342.3 2.1 convolution_add_fusion.13
  352.7 6.2 %maximum_convert_fusion.2 = bf16[4,512,2048]{2,1,0:T(8,128)(2,1)} fusion(f32[512]{0:T(512)S(1)} %iota_convert_fusion.2, f32[4,2048]{1,0:T(4,128)S(1)} %bitcast.105), kind=kLoop, calls=%fused_computation.clone.1 | loop fusion | flops 20971520 | bytes 8423424 | tf_op jit(solution)/shard_map/while/body/eval_jaxpr/convert_element_type | solution.py:60
  363.0 2.1 convolution_add_fusion.12
  370.9 2.1 convolution_add_fusion.14
  377.2 6.2 %maximum_convert_fusion.2 = bf16[4,512,2048]{2,1,0:T(8,128)(2,1)} fusion(f32[512]{0:T(512)S(1)} %iota_convert_fusion.2, f32[4,2048]{1,0:T(4,128)S(1)} %bitcast.105), kind=kLoop, calls=%fused_computation.clone.1 | loop fusion | flops 20971520 | bytes 8423424 | tf_op jit(solution)/shard_map/while/body/eval_jaxpr/convert_element_type | solution.py:60
  387.5 2.1 convolution_add_fusion.12
  391.3 2.1 convolution_add_fusion.13
  395.4 2.1 convolution_add_fusion.14
  401.7 6.2 %maximum_convert_fusion.2 = bf16[4,512,2048]{2,1,0:T(8,128)(2,1)} fusion(f32[512]{0:T(512)S(1)} %iota_convert_fusion.2, f32[4,2048]{1,0:T(4,128)S(1)} %bitcast.105), kind=kLoop, calls=%fused_computation.clone.1 | loop fusion | flops 20971520 | bytes 8423424 | tf_op jit(solution)/shard_map/while/body/eval_jaxpr/convert_element_type | solution.py:60
  415.8 2.1 convolution_add_fusion.13
  426.2 6.2 %maximum_convert_fusion.2 = bf16[4,512,2048]{2,1,0:T(8,128)(2,1)} fusion(f32[512]{0:T(512)S(1)} %iota_convert_fusion.2, f32[4,2048]{1,0:T(4,128)S(1)} %bitcast.105), kind=kLoop, calls=%fused_computation.clone.1 | loop fusion | flops 20971520 | bytes 8423424 | tf_op jit(solution)/shard_map/while/body/eval_jaxpr/convert_element_type | solution.py:60
  436.5 2.1 convolution_add_fusion.12
  440.3 2.1 convolution_add_fusion.13
  450.8 6.2 %maximum_convert_fusion.2 = bf16[4,512,2048]{2,1,0:T(8,128)(2,1)} fusion(f32[512]{0:T(512)S(1)} %iota_convert_fusion.2, f32[4,2048]{1,0:T(4,128)S(1)} %bitcast.105), kind=kLoop, calls=%fused_computation.clone.1 | loop fusion | flops 20971520 | bytes 8423424 | tf_op jit(solution)/shard_map/while/body/eval_jaxpr/convert_element_type | solution.py:60
  461.0 2.1 convolution_add_fusion.12
  475.2 6.2 %maximum_convert_fusion.2 = bf16[4,512,2048]{2,1,0:T(8,128)(2,1)} fusion(f32[512]{0:T(512)S(1)} %iota_convert_fusion.2, f32[4,2048]{1,0:T(4,128)S(1)} %bitcast.105), kind=kLoop, calls=%fused_computation.clone.1 | loop fusion | flops 20971520 | bytes 8423424 | tf_op jit(solution)/shard_map/while/body/eval_jaxpr/convert_element_type | solution.py:60
  489.3 2.1 convolution_add_fusion.13
  499.8 6.2 %maximum_convert_fusion.2 = bf16[4,512,2048]{2,1,0:T(8,128)(2,1)} fusion(f32[512]{0:T(512)S(1)} %iota_convert_fusion.2, f32[4,2048]{1,0:T(4,128)S(1)} %bitcast.105), kind=kLoop, calls=%fused_computation.clone.1 | loop fusion | flops 20971520 | bytes 8423424 | tf_op jit(solution)/shard_map/while/body/eval_jaxpr/convert_element_type | solution.py:60
  510.0 2.1 convolution_add_fusion.12
  517.9 2.1 convolution_add_fusion.14
  524.3 6.2 %maximum_convert_fusion.2 = bf16[4,512,2048]{2,1,0:T(8,128)(2,1)} fusion(f32[512]{0:T(512)S(1)} %iota_convert_fusion.2, f32[4,2048]{1,0:T(4,128)S(1)} %bitcast.105), kind=kLoop, calls=%fused_computation.clone.1 | loop fusion | flops 20971520 | bytes 8423424 | tf_op jit(solution)/shard_map/while/body/eval_jaxpr/convert_element_type | solution.py:60
  534.5 2.1 convolution_add_fusion.12
  542.4 2.1 convolution_add_fusion.14
  (233 shorter events, 106.8 us)
Async XLA Ops:
  6.5 146.0 %all-gather.2.cloned.1.call-start = ((), (), s32[]{:S(2)}) async-start(), calls=%async_computation | async-start | bytes 17301504 | tf_op jit(solution)/shard_map/all_gather | solution.py:107
  544.6 0.7 copy-start
Sparse Core Ops, SparseCore 0:
  44.5 108.0 all-gather.1
where the time goes:
time: 556 us; the launch traced here: 552 us
  matrix products  138 us (25%)
  loops' own time  131 us (24%)
  waiting for transfers between devices  107 us (19%)
  other arithmetic  106 us (19%)
  blocking collectives  31.7 us (6%)
  local copies, waits for them, and re-layouts  23.8 us (4%)
  between operations  14.1 us (3%)
    dot_general x64, matrix products, advance(): jnp.dot(window, weights[member], preferred_element_type=jnp.float32)  137 us
    another operation x1, loops' own time, accumulate_rows(): lax.scan(advance, total, (blocks, start_groups, jnp.arange(turns, dtype=j...  131 us
    all_gather x1, waiting for transfers between devices, body(): lax.all_gather(slab, ('segment', 'angle'), axis=0, tiled=True)  107 us
    convert_element_type x16, other arithmetic, hat_block(): return weight.astype(jnp.bfloat16)  99 us
    all_gather x1, blocking collectives, body(): slab = lax.all_gather(filtered, 'tile', axis=1, tiled=True)  31.7 us
  transfers between devices with their start and end apart: 1, of which 1 were waited for; matrix products, arithmetic and copies ran while one was open for 0% of the time, Pallas kernels for 0%

commit v1 on v0

--- a/solution.py
+++ b/solution.py
@@ -104,7 +104,12 @@
     slab = lax.all_gather(filtered, "tile", axis=1, tiled=True)
     volume = accumulate_rows(
         empty,
-        lax.all_gather(slab, ("segment", "angle"), axis=0, tiled=True),
+        jnp.concatenate(
+            lax.all_to_all(
+                jnp.stack([slab] * lax.axis_size(("segment", "angle"))), ("segment", "angle"), 0, 0
+            ),
+            axis=0,
+        ),
         own_starts,
         row_first,
         angle_total,

time: 556 us -> 829 us (1.49)
  waiting for transfers between devices: 107 us -> 379 us
  starting transfers between devices: 0.01 us -> 15.8 us
  between operations: 14.1 us -> 0.77 us
    all_to_all x0 -> x1, waiting for transfers between devices: none -> 379 us  [body(): lax.all_to_all(jnp.stack([slab] * lax.axis_size(('segment', 'angle'))), (...]
    all_gather x1 -> x0, waiting for transfers between devices: 107 us -> none  [body(): lax.all_gather(slab, ('segment', 'angle'), axis=0, tiled=True)]
    all_to_all x0 -> x1, starting transfers between devices: none -> 15.8 us  [body(): lax.all_to_all(jnp.stack([slab] * lax.axis_size(('segment', 'angle'))), (...]
where the time goes in v1:
time: 829 us; the launch traced here: 825 us
  waiting for transfers between devices  379 us (46%)
  matrix products  138 us (17%)
  loops' own time  127 us (15%)
  other arithmetic  106 us (13%)
  blocking collectives  31.6 us (4%)
  local copies, waits for them, and re-layouts  28 us (3%)
  starting transfers between devices  15.8 us (2%)
    all_to_all x1, waiting for transfers between devices, body(): lax.all_to_all(jnp.stack([slab] * lax.axis_size(('segment', 'angle'))), (...  379 us
    dot_general x64, matrix products, advance(): jnp.dot(window, weights[member], preferred_element_type=jnp.float32)  137 us
    another operation x1, loops' own time, accumulate_rows(): lax.scan(advance, total, (blocks, start_groups, jnp.arange(turns, dtype=j...  127 us
    convert_element_type x16, other arithmetic, hat_block(): return weight.astype(jnp.bfloat16)  98.8 us
    all_gather x1, blocking collectives, body(): slab = lax.all_gather(filtered, 'tile', axis=1, tiled=True)  31.6 us
  transfers between devices with their start and end apart: 1, of which 1 were waited for; matrix products, arithmetic and copies ran while one was open for 0% of the time, Pallas kernels for 0%

profile of v1, /device:TPU:1, one launch (start us, length us, event | category | flops | bytes accessed | tf_op | source)
XLA Modules:
  0.0 825.3 jit_solution(8475007170512093489)
XLA Ops:
  5.0 31.6 %all_gather.3 = bf16[2,32,4096]{2,0,1:T(2,128)(2,1)S(1)} all-gather(bf16[2,4,4096]{2,0,1:T(2,128)(2,1)S(1)} %copy.6), channel_id=1, replica_groups=mesh['segment'=2,'angle'=16,'tile'=8] {'tile'}, dimensions={1}, use_global_device_ids=true | all-gather | bytes 589824 | tf_op jit(solution)/shard_map/all_gather | solution.py:104
  36.9 5.9 stack.2
  42.9 15.8 %all-to-all-start = ((bf16[32,2,32,4096]{3,2,1,0:T(8,128)(2,1)}), bf16[32,2,32,4096]{3,2,1,0:T(8,128)(2,1)}, u32[]{:S(2)}, u32[]{:S(2)}) async-start(bf16[32,2,32,4096]{3,2,1,0:T(8,128)(2,1)} %stack.2), calls=%async_computation | async-start | bytes 33554432 | tf_op jit(solution)/shard_map/all_to_all | solution.py:108
  59.5 378.6 %all-to-all-done = bf16[32,2,32,4096]{3,2,1,0:T(8,128)(2,1)} async-done(((bf16[32,2,32,4096]{3,2,1,0:T(8,128)(2,1)}), bf16[32,2,32,4096]{3,2,1,0:T(8,128)(2,1)}, u32[]{:S(2)}, u32[]{:S(2)}) %all-to-all-start) | async-done | bytes 16777248 | tf_op jit(solution)/shard_map/all_to_all | solution.py:108
  438.2 386.4 %while.14 = (s32[]{:T(128)}, f32[32,2048]{1,0:T(8,128)S(1)}, bf16[16,4,32,4096]{3,2,1,0:T(8,128)(2,1)}, s32[16,4]{1,0:T(8,128)S(1)}, s32[16]{0:T(128)S(1)}, /*in...) while((s32[]{:T(128)}, f32[32,2048]{1,0:T(8,128)S(1)}, ...), condition=%wide.region_2.3_spmd.clone, body=%wide.region_1.2_spmd.clone.sunk | while | flops 289753152 | bytes 19153716 | solution.py:79
  441.9 6.2 maximum_convert_fusion.2
  456.1 2.1 convolution_add_fusion.13
  460.2 2.1 convolution_add_fusion.14
  466.1 6.2 maximum_convert_fusion.2
  476.4 2.1 convolution_add_fusion.12
  480.3 2.1 convolution_add_fusion.13
  484.3 2.1 convolution_add_fusion.14
  490.2 6.2 maximum_convert_fusion.2
  500.6 2.1 convolution_add_fusion.12
  504.4 2.1 convolution_add_fusion.13
  508.5 2.1 convolution_add_fusion.14
  514.4 6.2 maximum_convert_fusion.2
  524.7 2.1 convolution_add_fusion.12
  528.6 2.1 convolution_add_fusion.13
  532.6 2.1 convolution_add_fusion.14
  538.5 6.2 maximum_convert_fusion.2
  562.7 6.2 maximum_convert_fusion.2
  586.8 6.2 maximum_convert_fusion.2
  611.0 6.2 maximum_convert_fusion.2
  621.3 2.1 convolution_add_fusion.12
  625.2 2.1 convolution_add_fusion.13
  635.1 6.2 maximum_convert_fusion.2
  645.5 2.1 convolution_add_fusion.12
  649.3 2.1 convolution_add_fusion.13
  653.4 2.1 convolution_add_fusion.14
  659.3 6.2 maximum_convert_fusion.2
  669.6 2.1 convolution_add_fusion.12
  677.5 2.1 convolution_add_fusion.14
  683.4 6.2 maximum_convert_fusion.2
  693.8 2.1 convolution_add_fusion.12
  697.6 2.1 convolution_add_fusion.13
  701.7 2.1 convolution_add_fusion.14
  707.6 6.2 maximum_convert_fusion.2
  731.7 6.2 maximum_convert_fusion.2
  755.9 6.2 maximum_convert_fusion.2
  766.2 2.1 convolution_add_fusion.12
  770.1 2.1 convolution_add_fusion.13
  774.1 2.1 convolution_add_fusion.14
  780.0 6.2 maximum_convert_fusion.2
  804.2 6.2 maximum_convert_fusion.2
  814.5 2.1 convolution_add_fusion.12
  818.4 2.1 convolution_add_fusion.13
  822.4 2.1 convolution_add_fusion.14
  (233 shorter events, 109.3 us)
Async XLA Ops:
  42.9 395.3 %all-to-all-start = ((bf16[32,2,32,4096]{3,2,1,0:T(8,128)(2,1)}), bf16[32,2,32,4096]{3,2,1,0:T(8,128)(2,1)}, u32[]{:S(2)}, u32[]{:S(2)}) async-start(bf16[32,2,32,4096]{3,2,1,0:T(8,128)(2,1)} %stack.2), calls=%async_computation | async-start | bytes 33554432 | tf_op jit(solution)/shard_map/all_to_all | solution.py:108
  824.6 0.7 copy-start
